TPU v7x, 256 devices: a whole 4x4x8 slice. The times are simulated.
256 devices in a mesh: row: 16 (over z_lo, y), col: 16 (over z_hi, x, core).
Axes of the slice: x: 4, y: 4, z: 8 (z_hi: 2, z_lo: 4; z = z_hi * 4 + z_lo), core: 2. Of those that a mesh axis runs over, the one named last changes fastest.
Arguments:
- features: bfloat16 [16384, 512], P(('row', 'col')), may hold values from -6 to 6
- w_first: bfloat16 [512, 512], replicated, may hold values from -0.25 to 0.25
- w_second: bfloat16 [512, 512], replicated, may hold values from -0.25 to 0.25
- block_index: int32 [16, 16, 64], P('row', 'col'), may hold values from 0 to 63, as said below
- block_count: int32 [16, 16], P('row', 'col'), may hold values from 0 to 16, as said below
- block_values: bfloat16 [16, 16, 64, 128, 128], P('row', 'col'), may hold values from -0.15625 to 0.15625
- cotangent: bfloat16 [16384, 512], P(('row', 'col')), may hold values from -0.046875 to 0.046875
Outputs:
- out_second: bfloat16 [16384, 512], P(('row', 'col'))
- grad_first: float32 [512, 512], replicated
- grad_second: float32 [512, 512], replicated
Inputs may be any that keep to these rules, and one draw needn't show every extreme that they name: `block_index`: in each tile the 64 slots name every block position p = r * 8 + c (block row r, block column c of the tile) once, in some order; the first block_count slots are the tile's nonzero blocks and the others are unused. `block_count`: nonzero blocks of each tile; in every draw some tile has exactly 16.
All inputs are finite; a program needn't handle non-finite values.
Results may differ from a plain program's by a relative error of at most 0.0061.
Values may be sent and summed in bfloat16 or wider, within the bound.
A program may use at most 64 MiB of HBM per device.

v0:
```python
import math
import jax
import jax.numpy as jnp
from jax import lax
from jax.sharding import PartitionSpec as P


def activate(v):
    return jax.nn.gelu(v, approximate=True)


def combine(tile_values, slot_index, slot_count, full_panel, flip):
    slots = slot_index.shape[0]
    block_size = tile_values.shape[-1]
    feat_width = full_panel.shape[1]
    in_blocks = full_panel.shape[0] // block_size
    if flip:
        col_blocks = slots // in_blocks
        out_blocks = col_blocks
    else:
        col_blocks = in_blocks
        out_blocks = slots // in_blocks
    group_size = math.gcd(slots, 32)
    panel_blocks = full_panel.reshape(in_blocks, block_size, feat_width)
    targets = jnp.arange(out_blocks, dtype=jnp.int32)
    offsets = jnp.arange(group_size, dtype=jnp.int32)

    def add_group(group_no, total):
        first_slot = group_no * group_size
        slot_ids = lax.dynamic_slice_in_dim(slot_index, first_slot, group_size, 0)
        group_values = lax.dynamic_slice_in_dim(tile_values, first_slot, group_size, 0)
        block_row = slot_ids // col_blocks
        block_col = slot_ids % col_blocks
        if flip:
            picked = panel_blocks[block_row]
            product = jnp.einsum(
                "sab,saf->sbf", group_values, picked, preferred_element_type=jnp.float32
            )
            target = block_col
        else:
            picked = panel_blocks[block_col]
            product = jnp.einsum(
                "sab,sbf->saf", group_values, picked, preferred_element_type=jnp.float32
            )
            target = block_row
        is_live = first_slot + offsets < slot_count
        onehot = ((target[None, :] == targets[:, None]) & is_live[None, :]).astype(jnp.float32)
        return total + jnp.einsum("os,saf->oaf", onehot, product, precision=lax.Precision.HIGHEST)

    groups = (slot_count + group_size - 1) // group_size
    total = lax.fori_loop(
        0, groups, add_group, jnp.zeros((out_blocks, block_size, feat_width), jnp.float32)
    )
    return total.reshape(out_blocks * block_size, feat_width)


def spread_rows(layer_input, tile_values, slot_index, slot_count):
    full_panel = lax.all_gather(layer_input, "row", axis=0, tiled=True)
    partial_value = combine(tile_values, slot_index, slot_count, full_panel, False)
    return lax.psum_scatter(partial_value, "col", scatter_dimension=0, tiled=True)


def spread_cols(layer_input, tile_values, slot_index, slot_count):
    full_panel = lax.all_gather(layer_input, "col", axis=0, tiled=True)
    partial_value = combine(tile_values, slot_index, slot_count, full_panel, True)
    return lax.psum_scatter(partial_value, "row", scatter_dimension=0, tiled=True)


def local(features, w_first, w_second, block_index, block_count, block_values, cotangent):
    slot_index = block_index[0, 0]
    slot_count = block_count[0, 0]
    tile_values = block_values[0, 0]
    first_linear = jnp.dot(features, w_first, preferred_element_type=jnp.float32).astype(
        jnp.bfloat16
    )
    first_sum = spread_cols(first_linear, tile_values, slot_index, slot_count)
    first_value, act_back = jax.vjp(activate, first_sum)
    first_active = first_value.astype(jnp.bfloat16)
    second_linear = jnp.dot(first_active, w_second, preferred_element_type=jnp.float32).astype(
        jnp.bfloat16
    )
    out_second = spread_rows(second_linear, tile_values, slot_index, slot_count).astype(
        jnp.bfloat16
    )
    back_second = spread_cols(cotangent, tile_values, slot_index, slot_count).astype(jnp.bfloat16)
    second_terms = jnp.einsum(
        "nf,ng->fg", first_active, back_second, preferred_element_type=jnp.float32
    )
    back_act = jnp.einsum("ng,fg->nf", back_second, w_second, preferred_element_type=jnp.float32)
    back_first = act_back(back_act)[0].astype(jnp.bfloat16)
    back_linear = spread_rows(back_first, tile_values, slot_index, slot_count).astype(jnp.bfloat16)
    first_terms = jnp.einsum("nf,ng->fg", features, back_linear, preferred_element_type=jnp.float32)
    grad_first, grad_second = lax.psum((first_terms, second_terms), ("row", "col"))
    return (out_second, grad_first, grad_second)


def solution(mesh):
    return jax.shard_map(
        local,
        mesh=mesh,
        in_specs=(
            P(("row", "col"), None),
            P(),
            P(),
            P("row", "col", None),
            P("row", "col"),
            P("row", "col", None, None, None),
            P(("row", "col"), None),
        ),
        out_specs=(P(("row", "col"), None), P(), P()),
        check_vma=False,
    )
```

profile of v0, /device:TPU:2, one launch (start us, length us, event | category | flops | bytes accessed | tf_op | source)
XLA Modules:
  0.0 914.7 jit_solution(1774365751613363130)
XLA Ops:
  10.7 58.8 %all-gather.5.cloned.1.call-done = bf16[1024,512]{1,0:T(8,128)(2,1)} async-done(((bf16[64,512]{1,0:T(8,128)(2,1)}), bf16[1024,512]{1,0:T(8,128)(2,1)}) %all-gather.5.cloned.1.call-update) | async-done | bytes 1048592 | tf_op jit(solution)/shard_map/all_gather | solution.py:64
  71.2 18.2 %while.52 = (s32[]{:T(128)}, f32[8,128,512]{2,0,1:T(8,128)}, s32[]{:T(128)}, s32[64]{0:T(128)}, s32[]{:T(128)}, /*index=5*/bf16[64,128,128]{2,1,0:T(8,128)(2,1)}...) while((s32[]{:T(128)}, f32[8,128,512]{2,0,1:T(8,128)}, ...), condition=%wide.region_1.2_spmd.clone, body=%wide.region_0.1_spmd.clone.sunk | while | flops 738724224 | bytes 42997128 | solution.py:51
  72.6 4.1 gather_fusion
  80.9 8.4 fusion.129
  89.4 4.3 copy.13
  93.8 29.6 %all-gather.9.cloned.1.call-done = bf16[1024,512]{1,0:T(8,128)(2,1)} async-done(((bf16[64,512]{1,0:T(8,128)(2,1)}), bf16[1024,512]{1,0:T(8,128)(2,1)}) %all-gather.9.cloned.1.call-update) | async-done | bytes 1048592 | tf_op jit(solution)/shard_map/all_gather | solution.py:64
  125.1 16.8 %while.54 = (s32[]{:T(128)}, f32[8,128,512]{2,0,1:T(8,128)}, s32[]{:T(128)}, s32[64]{0:T(128)S(1)}, s32[]{:T(128)}, /*index=5*/bf16[64,128,128]{2,1,0:T(8,128)(2...) while((s32[]{:T(128)}, f32[8,128,512]{2,0,1:T(8,128)}, ...), condition=%wide.region_7.8_spmd.clone, body=%wide.region_6.7_spmd.clone.sunk | while | flops 738724224 | bytes 34608496 | solution.py:51
  133.4 8.4 fusion.143
  141.8 4.2 copy.15
  146.1 64.5 %reduce-scatter.5.cloned.1.call-done = f32[64,512]{1,0:T(8,128)} async-done(((f32[1024,512]{1,0:T(8,128)}), f32[64,512]{1,0:T(8,128)}) %reduce-scatter.5.cloned.1.call-update) | async-done | bytes 131088 | tf_op jit(solution)/shard_map/reduce_scatter | solution.py:66
  210.6 87.3 %reduce-scatter.9.cloned.1.call-done = f32[64,512]{1,0:T(8,128)} async-done(((f32[1024,512]{1,0:T(8,128)}), f32[64,512]{1,0:T(8,128)}) %reduce-scatter.9.cloned.1.call-update) | async-done | bytes 131088 | tf_op jit(solution)/shard_map/reduce_scatter | solution.py:66
  301.7 75.4 %all-gather.11.cloned.1.call-done = bf16[1024,512]{1,0:T(8,128)(2,1)} async-done(((bf16[64,512]{1,0:T(8,128)(2,1)}), bf16[1024,512]{1,0:T(8,128)(2,1)}) %all-gather.11.cloned.1.call-update) | async-done | bytes 1048592 | tf_op jit(solution)/shard_map/all_gather | solution.py:58
  378.7 16.6 %while.55 = (s32[]{:T(128)}, f32[8,128,512]{2,0,1:T(8,128)}, s32[]{:T(128)}, s32[64]{0:T(128)S(1)}, s32[]{:T(128)}, /*index=5*/bf16[64,128,128]{2,1,0:T(8,128)(2...) while((s32[]{:T(128)}, f32[8,128,512]{2,0,1:T(8,128)}, ...), condition=%wide.region_10.11_spmd.clone, body=%wide.region_9.10_spmd.clone.sunk | while | flops 738724160 | bytes 34608360 | solution.py:51
  378.8 4.0 gather_fusion.3
  386.9 8.4 fusion.150
  395.4 4.2 copy.16
  399.6 58.9 %all-gather.7.cloned.1.call-done = bf16[1024,512]{1,0:T(8,128)(2,1)} async-done(((bf16[64,512]{1,0:T(8,128)(2,1)}), bf16[1024,512]{1,0:T(8,128)(2,1)}) %all-gather.7.cloned.1.call-update) | async-done | bytes 1048592 | tf_op jit(solution)/shard_map/all_gather | solution.py:58
  460.1 16.6 %while.53 = (s32[]{:T(128)}, f32[8,128,512]{2,0,1:T(8,128)}, s32[]{:T(128)}, s32[64]{0:T(128)S(1)}, s32[]{:T(128)}, /*index=5*/bf16[64,128,128]{2,1,0:T(8,128)(2...) while((s32[]{:T(128)}, f32[8,128,512]{2,0,1:T(8,128)}, ...), condition=%wide.region_4.5_spmd.clone, body=%wide.region_3.4_spmd.clone.sunk | while | flops 738724160 | bytes 34608360 | solution.py:51
  460.2 4.0 gather_fusion.1
  468.3 8.4 fusion.136
  476.8 4.3 copy.14
  482.5 65.9 %reduce-scatter.11.cloned.1.call-done = f32[64,512]{1,0:T(8,128)} async-done(((f32[1024,512]{1,0:T(8,128)}), f32[64,512]{1,0:T(8,128)}) %reduce-scatter.11.cloned.1.call-update) | async-done | bytes 131088 | tf_op jit(solution)/shard_map/reduce_scatter | solution.py:60
  550.6 85.9 %reduce-scatter.7.cloned.1.call-done = f32[64,512]{1,0:T(8,128)} async-done(((f32[1024,512]{1,0:T(8,128)}), f32[64,512]{1,0:T(8,128)}) %reduce-scatter.7.cloned.1.call-update) | async-done | bytes 131088 | tf_op jit(solution)/shard_map/reduce_scatter | solution.py:60
  638.0 265.3 %all-reduce.3.cloned.1.call-done = (f32[512,512]{0,1:T(8,128)}, f32[512,512]{1,0:T(8,128)}) async-done(((f32[512,512]{0,1:T(8,128)}, f32[512,512]{1,0:T(8,128)}), (f32[512,512]{0,1:T(8,128)}, f32[512,512]{1,0:T(8,128)})) %all-reduce.3.cloned.1.call-update) | async-done | bytes 2097168 | tf_op jit(solution)/shard_map/psum | solution.py:93
  (67 shorter events, 45.6 us)
Async XLA Ops:
  7.2 290.7 %copy-start = (bf16[512,512]{1,0:T(8,128)(2,1)S(1)}, bf16[512,512]{1,0:T(8,128)(2,1)}, u32[]{:S(2)}) copy-start(bf16[512,512]{1,0:T(8,128)(2,1)} %param.17) | copy-start | bytes 1572868
  7.2 62.3 %all-gather.5.cloned.1.call-start = ((), (), s32[]{:S(2)}) async-start(), calls=%async_computation.4 | async-start | bytes 1114112 | tf_op jit(solution)/shard_map/all_gather | solution.py:64
  9.2 114.2 %all-gather.9.cloned.1.call-start = ((), (), s32[]{:S(2)}) async-start(), calls=%async_computation.8 | async-start | bytes 1114112 | tf_op jit(solution)/shard_map/all_gather | solution.py:64
  10.0 200.6 %reduce-scatter.5.cloned.1.call-start = ((), (), s32[]{:S(2)}) async-start(), calls=%async_computation.5 | async-start | bytes 2228224 | tf_op jit(solution)/shard_map/reduce_scatter | solution.py:66
  72.6 4.2 copy-start.2
  89.4 35.7 %copy-start.3 = (bf16[64,128,128]{2,1,0:T(8,128)(2,1)S(1)}, bf16[64,128,128]{2,1,0:T(8,128)(2,1)}, u32[]{:S(2)}) copy-start(bf16[64,128,128]{2,1,0:T(8,128)(2,1)} %get-tuple-element.970) | copy-start | bytes 6291460
  89.4 35.7 %copy-start.5 = (s32[64]{0:T(128)S(1)}, s32[64]{0:T(128)}, u32[]{:S(2)}) copy-start(s32[64]{0:T(128)} %get-tuple-element.988) | copy-start | bytes 772
  93.7 204.2 %reduce-scatter.9.cloned.1.call-start = ((), (), s32[]{:S(2)}) async-start(), calls=%async_computation.9 | async-start | bytes 2228224 | tf_op jit(solution)/shard_map/reduce_scatter | solution.py:66
  146.0 231.1 %all-gather.11.cloned.1.call-start = ((), (), s32[]{:S(2)}) async-start(), calls=%async_computation.10 | async-start | bytes 1114112 | tf_op jit(solution)/shard_map/all_gather | solution.py:58
  299.8 158.6 %all-gather.7.cloned.1.call-start = ((), (), s32[]{:S(2)}) async-start(), calls=%async_computation.6 | async-start | bytes 1114112 | tf_op jit(solution)/shard_map/all_gather | solution.py:58
  301.7 246.7 %reduce-scatter.11.cloned.1.call-start = ((), (), s32[]{:S(2)}) async-start(), calls=%async_computation.11 | async-start | bytes 2228224 | tf_op jit(solution)/shard_map/reduce_scatter | solution.py:60
  399.6 236.9 %reduce-scatter.7.cloned.1.call-start = ((), (), s32[]{:S(2)}) async-start(), calls=%async_computation.7 | async-start | bytes 2228224 | tf_op jit(solution)/shard_map/reduce_scatter | solution.py:60
  476.8 4.4 copy-start.4
  476.8 4.4 copy-start.7
  476.8 71.6 %copy-start.6 = (bf16[64,512]{1,0:T(8,128)(2,1)S(1)}, bf16[64,512]{1,0:T(8,128)(2,1)}, u32[]{:S(2)}) copy-start(bf16[64,512]{1,0:T(8,128)(2,1)} %param.15) | copy-start | bytes 196612
  481.1 422.3 %all-reduce.3.cloned.1.call-start = ((), (), s32[]{:S(2)}) async-start(), calls=%async_computation.12 | async-start | bytes 4194304 | tf_op jit(solution)/shard_map/psum | solution.py:93
  481.1 427.0 %copy-start.1 = (bf16[512,512]{1,0:T(8,128)(2,1)S(1)}, bf16[512,512]{1,0:T(8,128)(2,1)}, u32[]{:S(2)}) copy-start(bf16[512,512]{1,0:T(8,128)(2,1)} %param.17) | copy-start | bytes 1572868
Sparse Core Ops, SparseCore 0:
  11.3 58.1 all-gather.4
  72.2 51.1 all-gather.8
  126.0 84.6 reduce-scatter.4
  213.0 84.8 reduce-scatter.8
  300.1 76.9 all-gather.10
  379.3 79.1 all-gather.6
  462.7 85.6 reduce-scatter.10
  552.6 83.7 reduce-scatter.6
  642.6 260.7 all-reduce.2
where the time goes:
time: 915 us
  waiting for transfers between devices  792 us (87%)
  matrix products  56.7 us (6%)
  local copies, waits for them, and re-layouts  44.5 us (5%)
  between operations  14.6 us (2%)
    psum x1, waiting for transfers between devices, local(): lax.psum((first_terms, second_terms), ('row', 'col'))  265 us
    reduce_scatter x2, waiting for transfers between devices, spread_cols(): lax.psum_scatter(partial_value, 'row', scatter_dimension=0, tiled=True)  152 us
    reduce_scatter x2, waiting for transfers between devices, spread_rows(): lax.psum_scatter(partial_value, 'col', scatter_dimension=0, tiled=True)  152 us
    all_gather x2, waiting for transfers between devices, spread_rows(): full_panel = lax.all_gather(layer_input, 'row', axis=0, tiled=True)  134 us
    all_gather x2, waiting for transfers between devices, spread_cols(): full_panel = lax.all_gather(layer_input, 'col', axis=0, tiled=True)  88.4 us
    dot_general x4, matrix products, add_group(): jnp.einsum('os,saf->oaf', onehot, product, precision=lax.Precision.HIGHEST)  33.7 us
  transfers between devices with their start and end apart: 9, of which 9 were waited for; matrix products, arithmetic and copies ran while one was open for 11% of the time, Pallas kernels for 0%

commit v1 on v0

--- a/solution.py
+++ b/solution.py
@@ -3,6 +3,7 @@
 import jax.numpy as jnp
 from jax import lax
 from jax.sharding import PartitionSpec as P
+from jax.lax import all_to_all, axis_size
 
 
 def activate(v):
@@ -55,7 +56,10 @@
 
 
 def spread_rows(layer_input, tile_values, slot_index, slot_count):
-    full_panel = lax.all_gather(layer_input, "row", axis=0, tiled=True)
+    everything = jnp.stack([layer_input for _ in range(axis_size("row"))])
+    full_panel = jnp.concatenate(
+        all_to_all(everything, axis_name="row", split_axis=0, concat_axis=0), axis=0
+    )
     partial_value = combine(tile_values, slot_index, slot_count, full_panel, False)
     return lax.psum_scatter(partial_value, "col", scatter_dimension=0, tiled=True)
 

time: 915 us -> 810 us (0.89)
  waiting for transfers between devices: 792 us -> 673 us
  starting transfers between devices: 0.37 us -> 15.8 us
    all_gather x2 -> x0, waiting for transfers between devices: 134 us -> none  [spread_rows(): full_panel = lax.all_gather(layer_input, 'row', axis=0, tiled=True)]
    all_to_all x0 -> x2, waiting for transfers between devices: none -> 16.5 us  [spread_rows(): all_to_all(everything, axis_name='row', split_axis=0, concat_axis=0)]
    all_to_all x0 -> x2, starting transfers between devices: none -> 15.5 us  [spread_rows(): all_to_all(everything, axis_name='row', split_axis=0, concat_axis=0)]
  transfers between devices with their start and end apart: 9 -> 9, of which waited for: 9 -> 8; matrix products, arithmetic and copies ran while one was open for 11% -> 12% of each run, Pallas kernels for 0% -> 0%
where the time goes in v1:
time: 810 us; the launch traced here: 809 us
  waiting for transfers between devices  673 us (83%)
  matrix products  55.2 us (7%)
  local copies, waits for them, and re-layouts  44.2 us (5%)
  starting transfers between devices  15.8 us (2%)
  between operations  14.9 us (2%)
    psum x1, waiting for transfers between devices, local(): lax.psum((first_terms, second_terms), ('row', 'col'))  265 us
    reduce_scatter x2, waiting for transfers between devices, spread_cols(): lax.psum_scatter(partial_value, 'row', scatter_dimension=0, tiled=True)  152 us
    reduce_scatter x2, waiting for transfers between devices, spread_rows(): lax.psum_scatter(partial_value, 'col', scatter_dimension=0, tiled=True)  150 us
    all_gather x2, waiting for transfers between devices, spread_cols(): full_panel = lax.all_gather(layer_input, 'col', axis=0, tiled=True)  88.4 us
    dot_general x4, matrix products, add_group(): jnp.einsum('os,saf->oaf', onehot, product, precision=lax.Precision.HIGHEST)  33.8 us
    while x4, local copies, waits for them, and re-layouts, combine(): lax.fori_loop(0, groups, add_group, jnp.zeros((out_blocks, block_size, fe...  16.9 us
    all_to_all x2, waiting for transfers between devices, spread_rows(): all_to_all(everything, axis_name='row', split_axis=0, concat_axis=0)  16.5 us
  transfers between devices with their start and end apart: 9, of which 8 were waited for; matrix products, arithmetic and copies ran while one was open for 12% of the time, Pallas kernels for 0%

profile of v1, /device:TPU:2, one launch (start us, length us, event | category | flops | bytes accessed | tf_op | source)
XLA Modules:
  0.0 808.9 jit_solution(16226147788096159250)
XLA Ops:
  10.7 58.8 %all-gather.3.cloned.1.call-done = bf16[1024,512]{1,0:T(8,128)(2,1)} async-done(((bf16[64,512]{1,0:T(8,128)(2,1)}), bf16[1024,512]{1,0:T(8,128)(2,1)}) %all-gather.3.cloned.1.call-update) | async-done | bytes 1048592 | tf_op jit(solution)/shard_map/all_gather | solution.py:68
  71.2 18.2 %while.52 = (s32[]{:T(128)}, f32[8,128,512]{2,0,1:T(8,128)}, s32[]{:T(128)}, s32[64]{0:T(128)}, s32[]{:T(128)}, /*index=5*/bf16[64,128,128]{2,1,0:T(8,128)(2,1)}...) while((s32[]{:T(128)}, f32[8,128,512]{2,0,1:T(8,128)}, ...), condition=%wide.region_1.2_spmd.clone, body=%wide.region_0.1_spmd.clone.sunk | while | flops 738724224 | bytes 42997128 | solution.py:52
  72.7 4.1 gather_fusion
  80.9 8.5 %fusion.129 = f32[8,128,512]{2,0,1:T(8,128)} fusion(f32[8,128,512]{2,0,1:T(8,128)} %get-tuple-element.831, f32[32,128,512]{2,1,0:T(8,128)S(1)} %fusion.127, s32[32]{0:T(128)S(1)} %get-tuple-element.791, pred[32]{0:T(512)(128)(4,1)S(1)} %fusion.128), kind=kOutput, calls=%fused_computation.14.clone.1 | convolution fusion | flops 201851392 | bytes 12583072 | tf_op jit(solution)/shard_map/while/body/os,saf->oaf/dot_general | solution.py:49
  89.4 4.3 copy.13
  93.8 29.6 %all-gather.5.cloned.1.call-done = bf16[1024,512]{1,0:T(8,128)(2,1)} async-done(((bf16[64,512]{1,0:T(8,128)(2,1)}), bf16[1024,512]{1,0:T(8,128)(2,1)}) %all-gather.5.cloned.1.call-update) | async-done | bytes 1048592 | tf_op jit(solution)/shard_map/all_gather | solution.py:68
  125.1 16.7 %while.54 = (s32[]{:T(128)}, f32[8,128,512]{2,0,1:T(8,128)}, s32[]{:T(128)}, s32[64]{0:T(128)S(1)}, s32[]{:T(128)}, /*index=5*/bf16[64,128,128]{2,1,0:T(8,128)(2...) while((s32[]{:T(128)}, f32[8,128,512]{2,0,1:T(8,128)}, ...), condition=%wide.region_7.8_spmd.clone, body=%wide.region_6.7_spmd.clone.sunk | while | flops 738724224 | bytes 34608496 | solution.py:52
  125.3 4.0 gather_fusion.2
  133.4 8.4 %fusion.143 = f32[8,128,512]{2,0,1:T(8,128)} fusion(f32[8,128,512]{2,0,1:T(8,128)} %get-tuple-element.897, f32[32,128,512]{2,1,0:T(8,128)S(1)} %fusion.141, s32[32]{0:T(128)S(1)} %get-tuple-element.809, pred[32]{0:T(512)(128)(4,1)S(1)} %fusion.142), kind=kOutput, calls=%fused_computation.54.clone.1 | convolution fusion | flops 201851392 | bytes 12583072 | tf_op jit(solution)/shard_map/while/body/os,saf->oaf/dot_general | solution.py:49
  141.8 4.2 copy.15
  146.0 64.6 %reduce-scatter.5.cloned.1.call-done = f32[64,512]{1,0:T(8,128)} async-done(((f32[1024,512]{1,0:T(8,128)}), f32[64,512]{1,0:T(8,128)}) %reduce-scatter.5.cloned.1.call-update) | async-done | bytes 131088 | tf_op jit(solution)/shard_map/reduce_scatter | solution.py:70
  210.6 87.3 %reduce-scatter.9.cloned.1.call-done = f32[64,512]{1,0:T(8,128)} async-done(((f32[1024,512]{1,0:T(8,128)}), f32[64,512]{1,0:T(8,128)}) %reduce-scatter.9.cloned.1.call-update) | async-done | bytes 131088 | tf_op jit(solution)/shard_map/reduce_scatter | solution.py:70
  304.1 16.5 %all-to-all-done.1 = bf16[16,64,512]{2,1,0:T(8,128)(2,1)S(1)} async-done(((bf16[16,64,512]{2,1,0:T(8,128)(2,1)}), bf16[16,64,512]{2,1,0:T(8,128)(2,1)S(1)}, u32[]{:S(2)}, u32[]{:S(2)}) %all-to-all-start.1) | async-done | bytes 1048608 | tf_op jit(solution)/shard_map/all_to_all | solution.py:61
  321.7 11.9 %all-to-all-start = ((bf16[16,64,512]{2,1,0:T(8,128)(2,1)}), bf16[16,64,512]{2,1,0:T(8,128)(2,1)S(1)}, u32[]{:S(2)}, u32[]{:S(2)}) async-start(bf16[16,64,512]{2,1,0:T(8,128)(2,1)} %stack.4), calls=%async_computation.1 | async-start | bytes 2097152 | tf_op jit(solution)/shard_map/all_to_all | solution.py:61
  335.3 15.7 %while.55 = (s32[]{:T(128)}, f32[8,128,512]{2,0,1:T(8,128)}, s32[]{:T(128)}, s32[64]{0:T(128)S(1)}, s32[]{:T(128)}, /*index=5*/bf16[64,128,128]{2,1,0:T(8,128)(2...) while((s32[]{:T(128)}, f32[8,128,512]{2,0,1:T(8,128)}, ...), condition=%wide.region_10.11_spmd.clone, body=%wide.region_9.10_spmd.clone.sunk | while | flops 738724160 | bytes 34608360 | solution.py:52
  338.2 3.8 fusion.148
  342.6 8.4 %fusion.150 = f32[8,128,512]{2,0,1:T(8,128)} fusion(f32[8,128,512]{2,0,1:T(8,128)} %get-tuple-element.930, f32[32,128,512]{2,1,0:T(8,128)S(1)} %fusion.148, s32[32]{0:T(128)S(1)} %get-tuple-element.818, pred[32]{0:T(512)(128)(4,1)S(1)} %fusion.149), kind=kOutput, calls=%fused_computation.74.clone.1 | convolution fusion | flops 201851392 | bytes 12583072 | tf_op jit(solution)/shard_map/while/body/os,saf->oaf/dot_general | solution.py:49
  351.0 4.2 copy.16
  356.9 15.7 %while.53 = (s32[]{:T(128)}, f32[8,128,512]{2,0,1:T(8,128)}, s32[]{:T(128)}, s32[64]{0:T(128)S(1)}, s32[]{:T(128)}, /*index=5*/bf16[64,128,128]{2,1,0:T(8,128)(2...) while((s32[]{:T(128)}, f32[8,128,512]{2,0,1:T(8,128)}, ...), condition=%wide.region_4.5_spmd.clone, body=%wide.region_3.4_spmd.clone.sunk | while | flops 738724160 | bytes 34608360 | solution.py:52
  364.2 8.4 %fusion.136 = f32[8,128,512]{2,0,1:T(8,128)} fusion(f32[8,128,512]{2,0,1:T(8,128)} %get-tuple-element.864, f32[32,128,512]{2,1,0:T(8,128)S(1)} %fusion.134, s32[32]{0:T(128)S(1)} %get-tuple-element.800, pred[32]{0:T(512)(128)(4,1)S(1)} %fusion.135), kind=kOutput, calls=%fused_computation.34.clone.1 | convolution fusion | flops 201851392 | bytes 12583072 | tf_op jit(solution)/shard_map/while/body/os,saf->oaf/dot_general | solution.py:49
  372.6 4.3 copy.14
  378.3 64.2 %reduce-scatter.11.cloned.1.call-done = f32[64,512]{1,0:T(8,128)} async-done(((f32[1024,512]{1,0:T(8,128)}), f32[64,512]{1,0:T(8,128)}) %reduce-scatter.11.cloned.1.call-update) | async-done | bytes 131088 | tf_op jit(solution)/shard_map/reduce_scatter | solution.py:64
  444.7 85.7 %reduce-scatter.7.cloned.1.call-done = f32[64,512]{1,0:T(8,128)} async-done(((f32[1024,512]{1,0:T(8,128)}), f32[64,512]{1,0:T(8,128)}) %reduce-scatter.7.cloned.1.call-update) | async-done | bytes 131088 | tf_op jit(solution)/shard_map/reduce_scatter | solution.py:64
  531.9 265.3 %all-reduce.3.cloned.1.call-done = (f32[512,512]{0,1:T(8,128)}, f32[512,512]{1,0:T(8,128)}) async-done(((f32[512,512]{0,1:T(8,128)}, f32[512,512]{1,0:T(8,128)}), (f32[512,512]{0,1:T(8,128)}, f32[512,512]{1,0:T(8,128)})) %all-reduce.3.cloned.1.call-update) | async-done | bytes 2097168 | tf_op jit(solution)/shard_map/psum | solution.py:97
  (67 shorter events, 47.6 us)
Async XLA Ops:
  7.2 290.7 %copy-start = (bf16[512,512]{1,0:T(8,128)(2,1)S(1)}, bf16[512,512]{1,0:T(8,128)(2,1)}, u32[]{:S(2)}) copy-start(bf16[512,512]{1,0:T(8,128)(2,1)} %param.17) | copy-start | bytes 1572868
  7.2 62.3 %all-gather.3.cloned.1.call-start = ((), (), s32[]{:S(2)}) async-start(), calls=%async_computation.6 | async-start | bytes 1114112 | tf_op jit(solution)/shard_map/all_gather | solution.py:68
  9.2 114.2 %all-gather.5.cloned.1.call-start = ((), (), s32[]{:S(2)}) async-start(), calls=%async_computation.9 | async-start | bytes 1114112 | tf_op jit(solution)/shard_map/all_gather | solution.py:68
  10.0 200.6 %reduce-scatter.5.cloned.1.call-start = ((), (), s32[]{:S(2)}) async-start(), calls=%async_computation.7 | async-start | bytes 2228224 | tf_op jit(solution)/shard_map/reduce_scatter | solution.py:70
  72.6 4.1 copy-start.2
  89.4 35.7 %copy-start.3 = (bf16[64,128,128]{2,1,0:T(8,128)(2,1)S(1)}, bf16[64,128,128]{2,1,0:T(8,128)(2,1)}, u32[]{:S(2)}) copy-start(bf16[64,128,128]{2,1,0:T(8,128)(2,1)} %get-tuple-element.968) | copy-start | bytes 6291460
  89.4 35.7 %copy-start.5 = (s32[64]{0:T(128)S(1)}, s32[64]{0:T(128)}, u32[]{:S(2)}) copy-start(s32[64]{0:T(128)} %get-tuple-element.988) | copy-start | bytes 772
  93.7 204.2 %reduce-scatter.9.cloned.1.call-start = ((), (), s32[]{:S(2)}) async-start(), calls=%async_computation.10 | async-start | bytes 2228224 | tf_op jit(solution)/shard_map/reduce_scatter | solution.py:70
  210.6 93.3 %copy-start.4 = (f32[64,512]{1,0:T(8,128)S(1)}, f32[64,512]{1,0:T(8,128)}, u32[]{:S(2)}) copy-start(f32[64,512]{1,0:T(8,128)} %reduce-scatter.5.cloned.1.call-done) | copy-start | bytes 393220
  300.3 20.4 %all-to-all-start.1 = ((bf16[16,64,512]{2,1,0:T(8,128)(2,1)}), bf16[16,64,512]{2,1,0:T(8,128)(2,1)S(1)}, u32[]{:S(2)}, u32[]{:S(2)}) async-start(bf16[16,64,512]{2,1,0:T(8,128)(2,1)} %stack.5), calls=%async_computation.4 | async-start | bytes 2097152 | tf_op jit(solution)/shard_map/all_to_all | solution.py:61
  321.7 33.5 %all-to-all-start = ((bf16[16,64,512]{2,1,0:T(8,128)(2,1)}), bf16[16,64,512]{2,1,0:T(8,128)(2,1)S(1)}, u32[]{:S(2)}, u32[]{:S(2)}) async-start(bf16[16,64,512]{2,1,0:T(8,128)(2,1)} %stack.4), calls=%async_computation.1 | async-start | bytes 2097152 | tf_op jit(solution)/shard_map/all_to_all | solution.py:61
  333.6 108.9 %reduce-scatter.11.cloned.1.call-start = ((), (), s32[]{:S(2)}) async-start(), calls=%async_computation.11 | async-start | bytes 2228224 | tf_op jit(solution)/shard_map/reduce_scatter | solution.py:64
  355.2 175.2 %reduce-scatter.7.cloned.1.call-start = ((), (), s32[]{:S(2)}) async-start(), calls=%async_computation.8 | async-start | bytes 2228224 | tf_op jit(solution)/shard_map/reduce_scatter | solution.py:64
  372.6 4.3 copy-start.7
  372.6 69.9 %copy-start.6 = (bf16[64,512]{1,0:T(8,128)(2,1)S(1)}, bf16[64,512]{1,0:T(8,128)(2,1)}, u32[]{:S(2)}) copy-start(bf16[64,512]{1,0:T(8,128)(2,1)} %param.15) | copy-start | bytes 196612
  376.9 420.3 %all-reduce.3.cloned.1.call-start = ((), (), s32[]{:S(2)}) async-start(), calls=%async_computation.12 | async-start | bytes 4194304 | tf_op jit(solution)/shard_map/psum | solution.py:97
  377.0 425.1 %copy-start.1 = (bf16[512,512]{1,0:T(8,128)(2,1)S(1)}, bf16[512,512]{1,0:T(8,128)(2,1)}, u32[]{:S(2)}) copy-start(bf16[512,512]{1,0:T(8,128)(2,1)} %param.17) | copy-start | bytes 1572868
Sparse Core Ops, SparseCore 0:
  11.3 58.1 all-gather.2
  72.2 51.1 all-gather.4
  126.0 84.6 reduce-scatter.4
  213.0 84.8 reduce-scatter.8
  355.3 87.1 reduce-scatter.10
  446.6 83.7 reduce-scatter.6
  536.5 260.6 all-reduce.2
